TPU v7x, 32 devices: a whole 2x2x4 slice. The times are simulated.
32 devices in a mesh: clips: 16 (over z, x, core), mlp: 2 (over y).
Axes of the slice: x: 2, y: 2, z: 4, core: 2. Of those that a mesh axis runs over, the one named last changes fastest.
Arguments:
- flat_params: bfloat16 [3804160], replicated
- w_fc1: bfloat16 [768, 3072], P(None, 'mlp'), may hold values from -0.21875 to 0.21875
- w_fc2: bfloat16 [3072, 768], P('mlp'), may hold values from -0.15625 to 0.15625
- w_up: bfloat16 [512, 2048], P(None, 'mlp'), may hold values from -0.25 to 0.25
- w_down: bfloat16 [2048, 512], P('mlp'), may hold values from -0.21875 to 0.21875
- patches: bfloat16 [9984, 768], P(('clips', 'mlp')), may hold values from -6 to 6
- clip_ids: int32 [49152], P(('clips', 'mlp')), may hold values from 0 to 2, as said below
- visible_index: int32 [9984], P(('clips', 'mlp')), may hold values from 0 to 1535, as said below
- cotangent: bfloat16 [49152, 512], P(('clips', 'mlp')), may hold values from -6 to 6
Outputs:
- decoded: bfloat16 [49152, 512], P(('clips', 'mlp'))
- input_grad: float32 [9984, 768], P(('clips', 'mlp'))
- param_grad: float32 [3804160], P('mlp')
- fc1_grad: float32 [768, 3072], P(None, 'mlp')
- fc2_grad: float32 [3072, 768], P('mlp')
- up_grad: float32 [512, 2048], P(None, 'mlp')
- down_grad: float32 [2048, 512], P('mlp')
Inputs may be any that keep to these rules, and one draw needn't show every extreme that they name: `clip_ids`: each buffer of 1536 patches is either one clip of 192 x 8 patches, all with id 0, or three clips of 512 patches with ids 0, 1, 2 in order; a clip's patch (t, f) is row t * 8 + f of it. Both kinds occur in every draw. `visible_index`: the 312 entries of a buffer are distinct and increasing positions within that buffer; a three-clip buffer has 104 of them in each clip.
All inputs are finite; a program needn't handle non-finite values.
Results may differ from a plain program's by a relative error of at most 0.028.
Values may be sent and summed in bfloat16 or wider, within the bound.
No kernel may reach another device: no remote copies, remote signals or barrier semaphores. Data moves between devices by JAX's collectives and lax.ppermute only.
A program may use at most 384 MiB of HBM per device.

v0:
```python
import math
import jax
import jax.numpy as jnp
from jax import lax
from jax.sharding import PartitionSpec as P

D = 768
HEADS = 12
DD = 512
DHEADS = 16
FREQ = 8
WIN = 4
LONG_FRAMES = 192
ROWS = 1536
VIS = 312
PARAMS = 3804160
EPSILON = 1e-06


def layer_norm(inputs, weight_gain):
    row_mean = jnp.mean(inputs, axis=-1, keepdims=True)
    centred = inputs - row_mean
    variance = jnp.mean(centred * centred, axis=-1, keepdims=True)
    return centred * lax.rsqrt(variance + EPSILON) * weight_gain


def exact_gelu(inputs):
    return jax.nn.gelu(inputs, approximate=False)


def unpack(flat):
    layout = ((D, 3 * D), (D, D), (D,), (D,), (D, DD), (DD,), (DD, 3 * DD), (DD, DD), (DD,), (DD,))
    members = []
    offset = 0
    for dims_of in layout:
        length = math.prod(dims_of)
        members.append(flat[offset : offset + length].reshape(dims_of))
        offset = offset + length
    return members


def to_windows(source, head_count):
    head_size = source.shape[-1] // head_count
    blocks = source.reshape(-1, LONG_FRAMES // WIN, WIN, FREQ // WIN, WIN, head_count, head_size)
    blocks = blocks.transpose(0, 1, 3, 2, 4, 5, 6)
    return blocks.reshape(-1, WIN * WIN, head_count, head_size)


def from_windows(source, buffers):
    blocks = source.reshape(buffers, LONG_FRAMES // WIN, FREQ // WIN, WIN, WIN, -1)
    blocks = blocks.transpose(0, 1, 3, 2, 4, 5)
    return blocks.reshape(buffers * ROWS, -1)


def matmul(left, right):
    return jnp.dot(left, right, preferred_element_type=jnp.float32)


def transposed(left, right):
    return lax.dot_general(
        left, right, (((0,), (0,)), ((), ())), preferred_element_type=jnp.float32
    )


def against(left, right):
    return lax.dot_general(
        left, right, (((1,), (1,)), ((), ())), preferred_element_type=jnp.float32
    )


def score_table(queries, key_rows, allowed):
    factor = 1.0 / math.sqrt(queries.shape[-1])
    scores = (
        jnp.einsum("bqhd,bkhd->bhqk", queries, key_rows, preferred_element_type=jnp.float32)
        * factor
    )
    if allowed is not None:
        scores = jnp.where(allowed, scores, -1e30)
    return scores


def attend_forward(queries, key_rows, val_rows, allowed):
    scores = score_table(queries, key_rows, allowed)
    highest = jnp.max(scores, axis=-1, keepdims=True)
    expont = jnp.exp(scores - highest)
    total_row = jnp.sum(expont, axis=-1, keepdims=True)
    attn_probs = (expont / total_row).astype(jnp.bfloat16)
    mixed = jnp.einsum("bhqk,bkhd->bqhd", attn_probs, val_rows, preferred_element_type=jnp.float32)
    return (mixed, highest + jnp.log(total_row))


def attend_backward(queries, key_rows, val_rows, allowed, log_total, mix_grad):
    factor = 1.0 / math.sqrt(queries.shape[-1])
    attn_probs = jnp.exp(score_table(queries, key_rows, allowed) - log_total)
    prob_grad = jnp.einsum(
        "bqhd,bkhd->bhqk", mix_grad, val_rows, preferred_element_type=jnp.float32
    )
    score_grad = (
        attn_probs * (prob_grad - jnp.sum(attn_probs * prob_grad, axis=-1, keepdims=True))
    ).astype(jnp.bfloat16)
    query_grad = (
        jnp.einsum("bhqk,bkhd->bqhd", score_grad, key_rows, preferred_element_type=jnp.float32)
        * factor
    )
    key_grad = (
        jnp.einsum("bhqk,bqhd->bkhd", score_grad, queries, preferred_element_type=jnp.float32)
        * factor
    )
    value_grad = jnp.einsum(
        "bhqk,bqhd->bkhd",
        attn_probs.astype(jnp.bfloat16),
        mix_grad,
        preferred_element_type=jnp.float32,
    )
    return (query_grad, key_grad, value_grad)


def shards(flat_params, w_fc1, w_fc2, w_up, w_down, patches, clip_ids, visible_index, cotangent):
    w_qkv, w_proj, g_one, g_two, w_embed, mask_token, w_dqkv, w_dproj, gd_one, gd_two = unpack(
        flat_params
    )
    buffers = patches.shape[0] // VIS
    rows_here = cotangent.shape[0]
    head_size = D // HEADS
    visible = visible_index.reshape(buffers, VIS)
    segment = jnp.take_along_axis(clip_ids.reshape(buffers, ROWS), visible, axis=1)
    allowed = (segment[:, :, None] == segment[:, None, :])[:, None]
    inputs = patches.astype(jnp.float32)
    enc_norm, norm_pull1 = jax.vjp(layer_norm, inputs, g_one.astype(jnp.float32))
    enc_norm = enc_norm.astype(jnp.bfloat16)
    enc_qkv = (
        matmul(enc_norm, w_qkv).astype(jnp.bfloat16).reshape(buffers, VIS, 3, HEADS, head_size)
    )
    enc_query, enc_key, enc_value = (enc_qkv[:, :, 0], enc_qkv[:, :, 1], enc_qkv[:, :, 2])
    enc_out, enc_lse = attend_forward(enc_query, enc_key, enc_value, allowed)
    enc_mix = enc_out.reshape(-1, D).astype(jnp.bfloat16)
    first = inputs + matmul(enc_mix, w_proj)
    enc_in2, norm_pull2 = jax.vjp(layer_norm, first, g_two.astype(jnp.float32))
    enc_in2 = enc_in2.astype(jnp.bfloat16)
    enc_all = lax.all_gather(enc_in2, "mlp", axis=0, tiled=True)
    enc_act, gelu_pull1 = jax.vjp(exact_gelu, matmul(enc_all, w_fc1))
    enc_hidden = enc_act.astype(jnp.bfloat16)
    second = first + lax.psum_scatter(
        matmul(enc_hidden, w_fc2), "mlp", scatter_dimension=0, tiled=True
    )
    second_low = second.astype(jnp.bfloat16)
    embedded = matmul(second_low, w_embed).astype(jnp.bfloat16)
    matches = visible[:, None, :] == jnp.arange(ROWS, dtype=jnp.int32)[None, :, None]
    filled = jnp.einsum(
        "brv,bvd->brd",
        matches.astype(jnp.bfloat16),
        embedded.reshape(buffers, VIS, DD),
        preferred_element_type=jnp.float32,
    )
    masked_rows = 1.0 - jnp.any(matches, axis=2).astype(jnp.float32)
    start = (filled + masked_rows[:, :, None] * mask_token.astype(jnp.float32)).reshape(
        rows_here, DD
    )
    dec_norm, norm_pull3 = jax.vjp(layer_norm, start, gd_one.astype(jnp.float32))
    dec_norm = dec_norm.astype(jnp.bfloat16)
    dec_qkv = matmul(dec_norm, w_dqkv).astype(jnp.bfloat16)
    dec_query = to_windows(dec_qkv[:, :DD], DHEADS)
    dec_key = to_windows(dec_qkv[:, DD : 2 * DD], DHEADS)
    dec_value = to_windows(dec_qkv[:, 2 * DD :], DHEADS)
    dec_out, dec_lse = attend_forward(dec_query, dec_key, dec_value, None)
    dec_mix = from_windows(dec_out, buffers).astype(jnp.bfloat16)
    middle = start + matmul(dec_mix, w_dproj)
    dec_in2, norm_pull4 = jax.vjp(layer_norm, middle, gd_two.astype(jnp.float32))
    dec_in2 = dec_in2.astype(jnp.bfloat16)
    rows_all = lax.all_gather(dec_in2, "mlp", axis=0, tiled=True)
    dec_act, gelu_pull2 = jax.vjp(exact_gelu, matmul(rows_all, w_up))
    dec_hidden = dec_act.astype(jnp.bfloat16)
    decoded_full = middle + lax.psum_scatter(
        matmul(dec_hidden, w_down).astype(jnp.bfloat16), "mlp", scatter_dimension=0, tiled=True
    ).astype(jnp.float32)
    upstream_all = lax.all_gather(cotangent, "mlp", axis=0, tiled=True)
    down_grad_part = transposed(dec_hidden, upstream_all)
    pre_grad = gelu_pull2(against(upstream_all, w_down))[0].astype(jnp.bfloat16)
    up_grad_part = transposed(rows_all, pre_grad)
    in2_grad = lax.psum_scatter(
        against(pre_grad, w_up).astype(jnp.bfloat16), "mlp", scatter_dimension=0, tiled=True
    ).astype(jnp.float32)
    decoded = decoded_full.astype(jnp.bfloat16)
    middle_part, gd_two_grad = norm_pull4(in2_grad)
    middle_grad = cotangent.astype(jnp.float32) + middle_part
    dec_branch = middle_grad.astype(jnp.bfloat16)
    dproj_grad = transposed(dec_mix, dec_branch)
    dec_mix_grad = to_windows(against(dec_branch, w_dproj).astype(jnp.bfloat16), DHEADS)
    dq_grad, dk_grad, dv_grad = attend_backward(
        dec_query, dec_key, dec_value, None, dec_lse, dec_mix_grad
    )
    dec_qkv_grad = jnp.concatenate(
        [
            from_windows(dq_grad, buffers),
            from_windows(dk_grad, buffers),
            from_windows(dv_grad, buffers),
        ],
        axis=1,
    ).astype(jnp.bfloat16)
    dqkv_weight_grad = transposed(dec_norm, dec_qkv_grad)
    start_part, gd_one_grad = norm_pull3(against(dec_qkv_grad, w_dqkv))
    start_grad = (middle_grad + start_part).reshape(buffers, ROWS, DD)
    mask_grad = jnp.sum(start_grad * masked_rows[:, :, None], axis=(0, 1))
    embed_grad = (
        jnp.take_along_axis(start_grad, visible[:, :, None], axis=1)
        .reshape(-1, DD)
        .astype(jnp.bfloat16)
    )
    w_embed_grad = transposed(second_low, embed_grad)
    second_grad = against(embed_grad, w_embed)
    out_grad = second_grad.astype(jnp.bfloat16)
    out_all = lax.all_gather(out_grad, "mlp", axis=0, tiled=True)
    fc2_grad_part = transposed(enc_hidden, out_all)
    fc_pre_grad = gelu_pull1(against(out_all, w_fc2))[0].astype(jnp.bfloat16)
    fc1_grad_part = transposed(enc_all, fc_pre_grad)
    enc_in2_grad = lax.psum_scatter(
        against(fc_pre_grad, w_fc1).astype(jnp.bfloat16), "mlp", scatter_dimension=0, tiled=True
    ).astype(jnp.float32)
    first_part, g_two_grad = norm_pull2(enc_in2_grad)
    first_grad = second_grad + first_part
    enc_branch = first_grad.astype(jnp.bfloat16)
    proj_grad = transposed(enc_mix, enc_branch)
    enc_mix_grad = (
        against(enc_branch, w_proj).astype(jnp.bfloat16).reshape(buffers, VIS, HEADS, head_size)
    )
    eq_grad, ek_grad, ev_grad = attend_backward(
        enc_query, enc_key, enc_value, allowed, enc_lse, enc_mix_grad
    )
    enc_qkv_grad = (
        jnp.stack([eq_grad, ek_grad, ev_grad], axis=2).reshape(-1, 3 * D).astype(jnp.bfloat16)
    )
    qkv_weight_grad = transposed(enc_norm, enc_qkv_grad)
    input_part, g_one_grad = norm_pull1(against(enc_qkv_grad, w_qkv))
    input_grad = first_grad + input_part
    members = [
        qkv_weight_grad,
        proj_grad,
        g_one_grad,
        g_two_grad,
        w_embed_grad,
        mask_grad,
        dqkv_weight_grad,
        dproj_grad,
        gd_one_grad,
        gd_two_grad,
    ]
    flat_grad = jnp.concatenate(
        [member.reshape(-1) for member in members]
        + [jnp.zeros((flat_params.shape[0] - PARAMS,), jnp.float32)]
    )
    shard_grad = lax.psum_scatter(
        flat_grad.astype(jnp.bfloat16), "mlp", scatter_dimension=0, tiled=True
    )
    param_grad, fc1_grad, fc2_grad, up_grad, down_grad = (
        lax.psum(shard_grad, "clips").astype(jnp.float32),
        lax.psum(fc1_grad_part.astype(jnp.bfloat16), "clips").astype(jnp.float32),
        lax.psum(fc2_grad_part.astype(jnp.bfloat16), "clips").astype(jnp.float32),
        lax.psum(up_grad_part.astype(jnp.bfloat16), "clips").astype(jnp.float32),
        lax.psum(down_grad_part.astype(jnp.bfloat16), "clips").astype(jnp.float32),
    )
    return (decoded, input_grad, param_grad, fc1_grad, fc2_grad, up_grad, down_grad)


def solution(mesh):
    placed = (
        P(),
        P(None, "mlp"),
        P("mlp", None),
        P(None, "mlp"),
        P("mlp", None),
        P(("clips", "mlp"), None),
        P(("clips", "mlp")),
        P(("clips", "mlp")),
        P(("clips", "mlp"), None),
    )
    return jax.shard_map(
        shards,
        mesh=mesh,
        in_specs=placed,
        out_specs=(
            P(("clips", "mlp"), None),
            P(("clips", "mlp"), None),
            P("mlp"),
            P(None, "mlp"),
            P("mlp", None),
            P(None, "mlp"),
            P("mlp", None),
        ),
        check_vma=False,
    )
```

profile of v0, /device:TPU:0, one launch (start us, length us, event | category | flops | bytes accessed | tf_op | source)
XLA Modules:
  0.0 1081.5 jit_solution(7096899038210828048)
XLA Ops:
  8.1 3.4 slice.69
  12.0 7.6 reshape.586
  19.6 4.5 convolution_convert_fusion.4
  24.1 3.7 copy.122
  44.2 14.8 %all_gather.12 = bf16[624,768]{1,0:T(8,128)(2,1)S(1)} all-gather(bf16[312,768]{1,0:T(8,128)(2,1)S(1)} %multiply_convert_fusion.8), channel_id=1, replica_groups=mesh['clips'=16,'mlp'=2] {'mlp'}, dimensions={0}, use_global_device_ids=true | all-gather | bytes 1437696 | tf_op jit(solution)/shard_map/all_gather | solution.py:140
  59.0 11.4 %multiply_convert_fusion.5 = (bf16[624,1536]{1,0:T(8,128)(2,1)S(1)}, f32[624,1536]{1,0:T(8,128)}, f32[624,1536]{1,0:T(8,128)}) fusion(bf16[624,768]{1,0:T(8,128)(2,1)S(1)} %all_gather.12, bf16[768,1536]{1,0:T(8,128)(2,1)S(1)} %copy-done), kind=kOutput, calls=%fused_computation.60 | convolution fusion | flops 1534500864 | bytes 12902400 | tf_op jit(solution)/shard_map/dot_general | solution.py:56
  83.8 4.3 reshape.594
  91.3 14.7 %reduce-scatter.5.cloned.1.call-done = f32[312,768]{1,0:T(8,128)} async-done(((f32[624,768]{1,0:T(8,128)}), f32[312,768]{1,0:T(8,128)}) %reduce-scatter.5.cloned.1.call-update) | async-done | bytes 958480 | tf_op jit(solution)/shard_map/reduce_scatter | solution.py:143
  108.1 4.4 fusion.84
  115.3 5.1 convolution_convert_fusion
  122.8 8.0 reshape.597
  130.7 9.1 copy.125
  139.8 8.1 reshape.599
  147.9 9.1 copy.126
  157.0 8.0 reshape.595
  165.0 9.1 copy.124
  174.0 12.6 %multiply_reduce_fusion.1 = (f32[96,16,16]{2,1,0:T(8,128)S(1)}, f32[96,16,16,16]{2,3,1,0:T(8,128)}) fusion(bf16[96,16,16,32]{3,1,2,0:T(8,128)(2,1)} %bitcast.143, bf16[96,16,16,32]{3,1,2,0:T(8,128)(2,1)} %bitcast.139), kind=kOutput, calls=%fused_computation.27 | convolution fusion | flops 25927680 | bytes 4816896 | tf_op jit(solution)/shard_map/bqhd,bkhd->bhqk/dot_general | solution.py:74
  186.6 7.5 fusion.6
  194.1 10.4 convert_bitcast_fusion.1
  204.5 8.0 copy.128
  212.5 9.1 convert_element_type.229
  225.0 3.5 convert_element_type.231
  228.5 3.4 fusion.85
  236.0 44.3 %all-gather.3.cloned.1.call-done = bf16[3072,512]{0,1:T(8,128)(2,1)} async-done(((bf16[1536,512]{0,1:T(8,128)(2,1)}), bf16[3072,512]{0,1:T(8,128)(2,1)}) %all-gather.3.cloned.1.call-update) | async-done | bytes 3145744 | tf_op jit(solution)/shard_map/all_gather | solution.py:170
  280.4 33.5 %multiply_convert_fusion.3 = (bf16[3072,1024]{1,0:T(8,128)(2,1)}, f32[3072,1024]{1,0:T(8,128)}, f32[3072,1024]{1,0:T(8,128)}) fusion(bf16[3072,512]{0,1:T(8,128)(2,1)} %all-gather.3.cloned.1.call-done, bf16[512,1024]{1,0:T(8,128)(2,1)} %param.12), kind=kOutput, calls=%fused_computation.10 | convolution fusion | flops 3425697792 | bytes 35651584 | tf_op jit(solution)/shard_map/dot_general | solution.py:56
  313.9 13.0 %all-gather.5.cloned.1.call-done = bf16[3072,512]{1,0:T(8,128)(2,1)} async-done(((bf16[1536,512]{1,0:T(8,128)(2,1)}), bf16[3072,512]{1,0:T(8,128)(2,1)}) %all-gather.5.cloned.1.call-update) | async-done | bytes 3145744 | tf_op jit(solution)/shard_map/all_gather | solution.py:176
  326.9 14.1 %add_convert_fusion = bf16[3072,1024]{1,0:T(8,128)(2,1)S(1)} fusion(f32[3072,1024]{1,0:T(8,128)} %get-tuple-element.58, f32[3072,1024]{1,0:T(8,128)} %get-tuple-element.83, bf16[3072,512]{1,0:T(8,128)(2,1)} %all-gather.5.cloned.1.call-done, bf16[1024,512]{1,0:T(8,128)(2,1)} %param.13), kind=kOutput, calls=%fused_computation.9 | convolution fusion | flops 3265265664 | bytes 35651584 | tf_op jit(solution)/shard_map/dot_general | solution.py:66
  343.6 4.8 convolution_convert_fusion.2
  352.8 9.2 convolution_convert_fusion.3
  362.1 29.9 %reduce-scatter.9.cloned.1.call-done = bf16[1536,512]{0,1:T(8,128)(2,1)} async-done(((bf16[3072,512]{0,1:T(8,128)(2,1)}), bf16[1536,512]{0,1:T(8,128)(2,1)}) %reduce-scatter.9.cloned.1.call-update) | async-done | bytes 1572880 | tf_op jit(solution)/shard_map/reduce_scatter | solution.py:180
  401.9 8.3 reshape.601
  410.3 5.1 copy.133
  415.4 10.5 convert_bitcast_fusion
  425.9 8.0 copy.141
  433.9 9.1 reshape.607
  446.4 3.5 reshape.608
  449.9 14.4 %multiply_reduce_fusion = (f32[96,16,16]{2,1,0:T(8,128)}, f32[96,16,16,16]{2,3,1,0:T(8,128)}) fusion(f32[96,16,16,16]{2,3,1,0:T(8,128)} %get-tuple-element.80, f32[96,16,16]{2,1,0:T(8,128)S(1)} %log_add_fusion, bf16[96,16,16,32]{3,1,2,0:T(8,128)(2,1)} %bitcast.146, bf16[96,16,16,32]{3,2,1,0:T(8,128)(2,1)} %bitcast.142), kind=kOutput, calls=%fused_computation.7 | convolution fusion | flops 26714112 | bytes 6488064 | tf_op jit(solution)/shard_map/bqhd,bkhd->bhqk/dot_general | solution.py:95
  464.4 10.1 multiply_convert_fusion.2
  474.5 8.5 fusion.11
  483.0 5.3 copy.138
  488.3 9.1 reshape.605
  500.7 3.5 reshape.606
  504.2 6.3 fusion.10
  510.5 5.3 copy.136
  515.8 9.1 reshape.603
  528.3 3.5 reshape.604
  540.6 7.7 multiply_reduce_fusion.4
  550.9 3.6 gather_fusion.1
  556.0 13.4 %all_gather.15 = bf16[624,768]{1,0:T(8,128)(2,1)S(1)} all-gather(bf16[312,768]{1,0:T(8,128)(2,1)S(1)} %get-tuple-element.88), channel_id=1, replica_groups=mesh['clips'=16,'mlp'=2] {'mlp'}, dimensions={0}, use_global_device_ids=true | all-gather | bytes 1437696 | tf_op jit(solution)/shard_map/all_gather | solution.py:212
  569.4 6.2 add_convert_fusion.1
  579.6 7.1 convolution_convert_fusion.8
  586.7 4.5 reshape.614
  605.7 4.3 multiply_reduce_fusion.2
  617.2 4.1 convolution_convert_fusion.1
  624.1 7.7 reshape.611
  645.5 13.4 %dynamic-update-slice.4 = bf16[3804160]{0:T(1024)(128)(2,1)} dynamic-update-slice(bf16[3804160]{0:T(1024)(128)(2,1)} %dynamic-update-slice.3, bf16[393216]{0:T(1024)(128)(2,1)} %bitcast.162, s32[]{} %constant.44) | dynamic-update-slice | bytes 1572868
  668.9 8.3 convolution_convert_fusion.11
  677.2 7.4 convolution_convert_fusion.10
  684.6 3.6 convolution_convert_fusion.5
  688.2 3.4 convolution_convert_fusion.6
  691.6 157.8 %all-reduce.5.cloned.1.call-done = bf16[3804160]{0:T(1024)(128)(2,1)} async-done(((bf16[3804160]{0:T(1024)(128)(2,1)}), bf16[3804160]{0:T(1024)(128)(2,1)}) %all-reduce.5.cloned.1.call-update) | async-done | bytes 7608336
  849.4 4.8 dynamic-slice.1
  859.5 201.2 %all-reduce.7.cloned.1.call-done = (bf16[1902080]{0:T(1024)(128)(2,1)}, bf16[768,1536]{1,0:T(8,128)(2,1)}, bf16[1536,768]{1,0:T(8,128)(2,1)}, bf16[512,1024]{1,0:T(8,128)(2,1)}, bf16[1024,512]{1,0:T(8,128)(2,1)}) async-done(((bf16[1902080]{0:T(1024)(128)(2,1)}, bf16[768,1536]{1,0:T(8,128)(2,1)}, bf16[1536,768]{1,0:T(8,128)(2,1)}, bf16[512,1024]{1,0:T(8,128)(2,1)}, bf16[1024,512]{1,0:T(8,128)(2,1)}), ...) | async-done | bytes 10619920 | tf_op jit(solution)/shard_map/psum | solution.py:255
  1060.7 5.1 convert_element_type.257
  (295 shorter events, 153.8 us)
Async XLA Ops:
  7.2 51.8 %copy-start = (bf16[768,1536]{1,0:T(8,128)(2,1)S(1)}, bf16[768,1536]{1,0:T(8,128)(2,1)}, u32[]{:S(2)}) copy-start(bf16[768,1536]{1,0:T(8,128)(2,1)} %param.10) | copy-start | bytes 7077892
  7.2 98.9 %reduce-scatter.5.cloned.1.call-start = ((), (), s32[]{:S(2)}) async-start(), calls=%async_computation.4 | async-start | bytes 2875392 | tf_op jit(solution)/shard_map/reduce_scatter | solution.py:143
  8.1 11.5 %copy-start.56 = (f32[768]{0:T(1024)}, f32[768]{0:T(1024)S(1)}, u32[]{:S(2)}) copy-start(f32[768]{0:T(1024)S(1)} %get-tuple-element.67) | copy-start | bytes 9220
  8.1 35.9 %copy-start.46 = (f32[768]{0:T(1024)}, f32[768]{0:T(1024)S(1)}, u32[]{:S(2)}) copy-start(f32[768]{0:T(1024)S(1)} %get-tuple-element.66) | copy-start | bytes 9220
  8.1 3.4 copy-start.16
  11.7 12.4 %copy-start.58 = (f32[312]{0:T(512)}, f32[312]{0:T(512)S(1)}, u32[]{:S(2)}) copy-start(f32[312]{0:T(512)S(1)} %broadcast_multiply_fusion.3) | copy-start | bytes 3748
  12.0 12.1 %copy-start.68 = (f32[312]{0:T(512)}, f32[312]{0:T(512)S(1)}, u32[]{:S(2)}) copy-start(f32[312]{0:T(512)S(1)} %fusion.61) | copy-start | bytes 3748
  12.0 12.1 %copy-start.66 = (f32[312]{0:T(512)}, f32[312]{0:T(512)S(1)}, u32[]{:S(2)}) copy-start(f32[312]{0:T(512)S(1)} %fusion.68) | copy-start | bytes 3748
  19.6 8.2 copy-start.72
  24.1 3.7 copy-start.1
  27.9 5.4 copy-start.73
  36.4 3.2 slice-start.2
  43.7 62.4 %copy-start.8 = (f32[312,768]{1,0:T(8,128)}, f32[312,768]{1,0:T(8,128)S(1)}, u32[]{:S(2)}) copy-start(f32[312,768]{1,0:T(8,128)S(1)} %get-tuple-element.75) | copy-start | bytes 2875396
  43.7 26.7 %copy-start.50 = (f32[312]{0:T(512)}, f32[312]{0:T(512)S(1)}, u32[]{:S(2)}) copy-start(f32[312]{0:T(512)S(1)} %broadcast_multiply_fusion.2) | copy-start | bytes 3748
  44.0 26.4 %copy-start.70 = (f32[312]{0:T(512)}, f32[312]{0:T(512)S(1)}, u32[]{:S(2)}) copy-start(f32[312]{0:T(512)S(1)} %multiply_reduce_fusion.8) | copy-start | bytes 3748
  44.0 26.4 %copy-start.60 = (f32[312]{0:T(512)}, f32[312]{0:T(512)S(1)}, u32[]{:S(2)}) copy-start(f32[312]{0:T(512)S(1)} %fusion.69) | copy-start | bytes 3748
  59.0 11.4 %copy-start.36 = (bf16[624,768]{1,0:T(8,128)(2,1)}, bf16[624,768]{1,0:T(8,128)(2,1)S(1)}, u32[]{:S(2)}) copy-start(bf16[624,768]{1,0:T(8,128)(2,1)S(1)} %all_gather.12) | copy-start | bytes 2875396
  59.0 12.7 %copy-start.77 = (bf16[1536,768]{1,0:T(8,128)(2,1)S(1)}, bf16[1536,768]{1,0:T(8,128)(2,1)}, u32[]{:S(2)}) copy-start(bf16[1536,768]{1,0:T(8,128)(2,1)} %param.11) | copy-start | bytes 7077892
  74.6 205.8 %all-gather.3.cloned.1.call-start = ((), (), s32[]{:S(2)}) async-start(), calls=%async_computation.5 | async-start | bytes 4718592 | tf_op jit(solution)/shard_map/all_gather | solution.py:170
  91.3 24.0 %copy-start.64 = (f32[512]{0:T(512)}, f32[512]{0:T(512)S(1)}, u32[]{:S(2)}) copy-start(f32[512]{0:T(512)S(1)} %get-tuple-element.64) | copy-start | bytes 6148
  91.3 21.2 %copy-start.62 = (f32[1536]{0:T(1024)}, f32[1536]{0:T(1024)S(1)}, u32[]{:S(2)}) copy-start(f32[1536]{0:T(1024)S(1)} %convert_subtract_fusion.1) | copy-start | bytes 18436
  112.5 8.0 copy-start.44
  115.3 5.1 copy-start.52
  186.6 7.5 copy-start.19
  194.1 10.4 copy-start.25
  221.6 6.9 copy-start.30
  235.3 91.6 %all-gather.5.cloned.1.call-start = ((), (), s32[]{:S(2)}) async-start(), calls=%async_computation.7 | async-start | bytes 4718592 | tf_op jit(solution)/shard_map/all_gather | solution.py:176
  236.0 156.0 %reduce-scatter.9.cloned.1.call-start = ((), (), s32[]{:S(2)}) async-start(), calls=%async_computation.8 | async-start | bytes 4718592 | tf_op jit(solution)/shard_map/reduce_scatter | solution.py:180
  326.9 16.8 %copy-start.79 = (bf16[512,1024]{1,0:T(8,128)(2,1)S(1)}, bf16[512,1024]{1,0:T(8,128)(2,1)}, u32[]{:S(2)}) copy-start(bf16[512,1024]{1,0:T(8,128)(2,1)} %param.12) | copy-start | bytes 3145732
  348.5 192.1 %reduce-scatter.7.cloned.1.call-start = ((), (), s32[]{:S(2)}) async-start(), calls=%async_computation.6 | async-start | bytes 4718592 | tf_op jit(solution)/shard_map/reduce_scatter | solution.py:173
  362.0 237.0 %reduce-scatter.11.cloned.1.call-start = ((), (), s32[]{:S(2)}) async-start(), calls=%async_computation.9 | async-start | bytes 1437696 | tf_op jit(solution)/shard_map/reduce_scatter | solution.py:216
  392.0 3.3 copy-start.3
  392.0 3.8 copy-start.10
  392.0 5.3 copy-start.13
  415.4 10.5 copy-start.6
  474.5 8.5 copy-start.5
  536.1 2.8 copy-start.53
  540.6 10.3 copy-start.74
  548.3 6.3 copy-start.26
  548.3 6.4 copy-start.75
  554.6 14.8 %copy-start.78 = (bf16[1536,768]{1,0:T(8,128)(2,1)S(1)}, bf16[1536,768]{1,0:T(8,128)(2,1)}, u32[]{:S(2)}) copy-start(bf16[1536,768]{1,0:T(8,128)(2,1)} %param.11) | copy-start | bytes 7077892
  569.4 6.2 copy-start.38
  579.5 269.9 %all-reduce.5.cloned.1.call-start = ((), (), s32[]{:S(2)}) async-start(), calls=%async_computation.10 | async-start | bytes 15216640
  579.6 11.6 %copy-start.41 = (bf16[312,768]{1,0:T(8,128)(2,1)S(1)}, bf16[312,768]{1,0:T(8,128)(2,1)}, u32[]{:S(2)}) copy-start(bf16[312,768]{1,0:T(8,128)(2,1)} %add_convert_fusion.3) | copy-start | bytes 1437700
  593.1 6.0 copy-start.9
  593.1 6.0 copy-start.47
  593.1 6.0 copy-start.51
  593.1 7.4 copy-start.71
  593.1 7.4 copy-start.61
  599.0 5.7 copy-start.18
  605.6 4.4 copy-start.22
  605.7 4.4 slice-start
  605.7 4.7 slice-start.1
  617.2 4.1 copy-start.24
  631.7 6.7 copy-start.69
  667.6 393.1 %all-reduce.7.cloned.1.call-start = ((), (), s32[]{:S(2)}) async-start(), calls=%async_computation.11 | async-start | bytes 21241856 | tf_op jit(solution)/shard_map/psum | solution.py:255
  668.9 8.3 copy-start.76
  677.2 7.4 copy-start.39
  677.2 7.4 copy-start.84
  684.6 3.6 copy-start.37
  684.6 3.6 copy-start.82
  1060.7 5.1 copy-start.28
  1065.7 2.8 copy-start.27
  1068.5 4.1 copy-start.34
  (33 other events, 65.5 us)
Sparse Core Ops, SparseCore 0:
  74.7 31.3 reduce-scatter.4
  235.4 44.9 all-gather.2
  281.9 44.9 all-gather.4
  348.6 43.3 reduce-scatter.8
  394.2 43.3 reduce-scatter.6
  579.6 19.3 reduce-scatter.10
  667.7 181.6 all-reduce.4
  854.4 206.2 all-reduce.6
where the time goes:
time: 1090 us; the launch traced here: 1080 us
  waiting for transfers between devices  464 us (43%)
  local copies, waits for them, and re-layouts  275 us (25%)
  matrix products  229 us (21%)
  other arithmetic  69.1 us (6%)
  blocking collectives  28.1 us (3%)
  between operations  16.1 us (1%)
    psum x1, waiting for transfers between devices, shards(): lax.psum(shard_grad, 'clips').astype(jnp.float32)  201 us
    unnamed x9, waiting for transfers between devices  159 us
    dot_general x8, matrix products, matmul(): return jnp.dot(left, right, preferred_element_type=jnp.float32)  72.3 us
    unnamed x193, local copies, waits for them, and re-layouts  59.8 us
    all_gather x1, waiting for transfers between devices, shards(): rows_all = lax.all_gather(dec_in2, 'mlp', axis=0, tiled=True)  44.3 us
    dot_general x9, matrix products, transposed(): lax.dot_general(left, right, (((0,), (0,)), ((), ())), preferred_element_...  39.4 us
    dot_general x9, matrix products, against(): lax.dot_general(left, right, (((1,), (1,)), ((), ())), preferred_element_...  37.4 us
    reshape x4, local copies, waits for them, and re-layouts, to_windows(): source.reshape(-1, LONG_FRAMES // WIN, WIN, FREQ // WIN, WIN, head_count,...  32.4 us
  transfers between devices with their start and end apart: 8, of which 7 were waited for; matrix products, arithmetic and copies ran while one was open for 23% of the time, Pallas kernels for 0%

commit v1 on v0

--- a/solution.py
+++ b/solution.py
@@ -15,6 +15,12 @@
 VIS = 312
 PARAMS = 3804160
 EPSILON = 1e-06
+
+
+def add_all(shard, axis):
+    blocks = lax.all_gather(shard, axis, axis=0, tiled=False)
+    summed = blocks.sum(axis=0)
+    return summed
 
 
 def layer_norm(inputs, weight_gain):
@@ -252,7 +258,7 @@
         flat_grad.astype(jnp.bfloat16), "mlp", scatter_dimension=0, tiled=True
     )
     param_grad, fc1_grad, fc2_grad, up_grad, down_grad = (
-        lax.psum(shard_grad, "clips").astype(jnp.float32),
+        add_all(shard_grad, "clips").astype(jnp.float32),
         lax.psum(fc1_grad_part.astype(jnp.bfloat16), "clips").astype(jnp.float32),
         lax.psum(fc2_grad_part.astype(jnp.bfloat16), "clips").astype(jnp.float32),
         lax.psum(up_grad_part.astype(jnp.bfloat16), "clips").astype(jnp.float32),

time: 1090 us -> 2240 us (2.06)
  other arithmetic: 69.1 us -> 703 us
  waiting for transfers between devices: 464 us -> 935 us
  local copies, waits for them, and re-layouts: 275 us -> 320 us
    reduce_sum x0 -> x1, other arithmetic: none -> 632 us  [add_all(): summed = blocks.sum(axis=0)]
    all_gather x0 -> x1, waiting for transfers between devices: none -> 573 us  [add_all(): blocks = lax.all_gather(shard, axis, axis=0, tiled=False)]
    psum x1, waiting for transfers between devices: 201 us -> 101 us  [shards(): lax.psum(fc1_grad_part.astype(jnp.bfloat16), 'clips').astype(jnp.float32)]
    unnamed x193 -> x200, local copies, waits for them, and re-layouts: 59.8 us -> 100 us
    unnamed x9 -> x10, waiting for transfers between devices: 159 us -> 158 us
  transfers between devices with their start and end apart: 8 -> 9, of which waited for: 7 -> 8; matrix products, arithmetic and copies ran while one was open for 23% -> 14% of each run, Pallas kernels for 0% -> 0%
where the time goes in v1:
time: 2240 us; the launch traced here: 2230 us
  waiting for transfers between devices  935 us (42%)
  other arithmetic  703 us (31%)
  local copies, waits for them, and re-layouts  320 us (14%)
  matrix products  230 us (10%)
  blocking collectives  28.5 us (1%)
    reduce_sum x1, other arithmetic, add_all(): summed = blocks.sum(axis=0)  632 us
    all_gather x1, waiting for transfers between devices, add_all(): blocks = lax.all_gather(shard, axis, axis=0, tiled=False)  573 us
    unnamed x10, waiting for transfers between devices  158 us
    psum x1, waiting for transfers between devices, shards(): lax.psum(fc1_grad_part.astype(jnp.bfloat16), 'clips').astype(jnp.float32)  101 us
    unnamed x200, local copies, waits for them, and re-layouts  100 us
    dot_general x8, matrix products, matmul(): return jnp.dot(left, right, preferred_element_type=jnp.float32)  71 us
  transfers between devices with their start and end apart: 9, of which 8 were waited for; matrix products, arithmetic and copies ran while one was open for 14% of the time, Pallas kernels for 0%

profile of v1, /device:TPU:0, one launch (start us, length us, event | category | flops | bytes accessed | tf_op | source)
XLA Modules:
  0.0 2232.4 jit_solution(11222896757157623585)
XLA Ops:
  21.2 7.6 reshape.586
  28.8 4.5 convolution_convert_fusion.4
  33.3 3.7 copy.122
  45.5 15.1 all_gather.18
  60.6 11.4 multiply_convert_fusion.5
  87.5 4.3 reshape.594
  93.0 14.7 reduce-scatter.5.cloned.1.call-done
  109.7 4.4 fusion.84
  116.9 5.1 convolution_convert_fusion
  124.4 8.0 reshape.599
  132.3 9.1 copy.126
  141.4 8.1 reshape.597
  149.5 9.1 copy.125
  158.5 8.0 reshape.595
  166.5 9.1 copy.124
  175.6 12.6 multiply_reduce_fusion.1
  188.1 7.5 fusion.6
  195.7 10.2 convert_bitcast_fusion.1
  205.9 8.0 copy.128
  213.9 9.1 convert_element_type.231
  226.4 3.5 convert_element_type.233
  237.4 44.3 %all-gather.6.cloned.1.call-done = bf16[3072,512]{0,1:T(8,128)(2,1)} async-done(((bf16[1536,512]{0,1:T(8,128)(2,1)}), bf16[3072,512]{0,1:T(8,128)(2,1)}) %all-gather.6.cloned.1.call-update) | async-done | bytes 3145744 | tf_op jit(solution)/shard_map/all_gather | solution.py:176
  281.7 33.8 %multiply_convert_fusion.3 = (bf16[3072,1024]{1,0:T(8,128)(2,1)}, f32[3072,1024]{1,0:T(8,128)}, f32[3072,1024]{1,0:T(8,128)}) fusion(bf16[3072,512]{0,1:T(8,128)(2,1)} %all-gather.6.cloned.1.call-done, bf16[512,1024]{1,0:T(8,128)(2,1)} %param.12), kind=kOutput, calls=%fused_computation.10 | convolution fusion | flops 3425697792 | bytes 35651584 | tf_op jit(solution)/shard_map/dot_general | solution.py:62
  315.5 12.7 all-gather.8.cloned.1.call-done
  328.2 14.1 add_convert_fusion
  345.0 4.8 convolution_convert_fusion.2
  354.1 9.2 convolution_convert_fusion.3
  363.4 29.9 %reduce-scatter.9.cloned.1.call-done = bf16[1536,512]{0,1:T(8,128)(2,1)} async-done(((bf16[3072,512]{0,1:T(8,128)(2,1)}), bf16[1536,512]{0,1:T(8,128)(2,1)}) %reduce-scatter.9.cloned.1.call-update) | async-done | bytes 1572880 | tf_op jit(solution)/shard_map/reduce_scatter | solution.py:186
  403.3 8.2 reshape.601
  411.4 5.1 copy.133
  416.6 10.5 convert_bitcast_fusion
  427.1 8.0 copy.141
  435.1 9.1 reshape.607
  447.6 3.5 reshape.608
  451.1 14.4 multiply_reduce_fusion
  465.5 10.3 multiply_convert_fusion.2
  475.9 6.7 fusion.10
  482.6 5.3 copy.136
  487.9 9.1 reshape.603
  500.3 3.6 reshape.604
  504.0 8.1 fusion.11
  512.1 5.3 copy.138
  517.4 9.1 reshape.605
  542.1 7.9 multiply_reduce_fusion.4
  552.7 3.6 gather_fusion.1
  557.8 13.4 all_gather.21
  571.2 6.2 add_convert_fusion.1
  585.5 6.5 convolution_convert_fusion.8
  592.0 4.7 reshape.614
  608.7 3.8 fusion.44
  612.6 4.0 multiply_reduce_fusion.2
  623.8 4.2 convolution_convert_fusion.1
  631.4 7.7 reshape.611
  639.1 3.5 constant_dynamic-update-slice_fusion.3
  647.1 13.4 dynamic-update-slice.4
  668.2 8.3 convolution_convert_fusion.10
  676.5 7.4 convolution_convert_fusion.11
  692.7 157.3 %all-reduce.5.cloned.1.call-done = bf16[3804160]{0:T(1024)(128)(2,1)} async-done(((bf16[3804160]{0:T(1024)(128)(2,1)}), bf16[3804160]{0:T(1024)(128)(2,1)}) %all-reduce.5.cloned.1.call-update) | async-done | bytes 7608336
  850.0 3.6 dynamic-slice.1
  853.6 44.2 %reshape.643 = bf16[1,1,1902080]{2,1,0:T(2,128)(2,1)} reshape(bf16[1902080]{0:T(1024)(128)(2,1)S(1)} %dynamic-slice.1) | data formatting | bytes 7608320
  903.2 100.5 %all-reduce.7.cloned.1.call-done = (bf16[768,1536]{1,0:T(8,128)(2,1)}, bf16[1536,768]{1,0:T(8,128)(2,1)}, bf16[512,1024]{1,0:T(8,128)(2,1)}, bf16[1024,512]{1,0:T(8,128)(2,1)}) async-done(((bf16[768,1536]{1,0:T(8,128)(2,1)}, bf16[1536,768]{1,0:T(8,128)(2,1)}, bf16[512,1024]{1,0:T(8,128)(2,1)}, bf16[1024,512]{1,0:T(8,128)(2,1)}), (bf16[768,1536]{1,0:T(8,128)(2,1)}, bf16[1536,768]{1,0:T(8,128)(2,1)}, ...) | async-done | bytes 6815760 | tf_op jit(solution)/shard_map/psum | solution.py:262
  1015.8 573.3 %all-gather.10.cloned.1.call-done = bf16[16,1,1902080]{2,1,0:T(2,128)(2,1)} async-done(((bf16[1,1,1902080]{2,1,0:T(2,128)(2,1)}), bf16[16,1,1902080]{2,1,0:T(2,128)(2,1)}) %all-gather.10.cloned.1.call-update) | async-done | bytes 60866576 | tf_op jit(solution)/shard_map/all_gather | solution.py:21
  1589.1 631.6 %reduce_sum.310 = bf16[1902080]{0:T(1024)(128)(2,1)} reduce(bf16[16,1,1902080]{2,1,0:T(2,128)(2,1)} %all-gather.10.cloned.1.call-done, bf16[]{:T(256)} %constant.91.clone.1), dimensions={0,1}, to_apply=%region_33.34 | reduce | flops 28531200 | bytes 64670720 | tf_op jit(solution)/shard_map/reduce_sum | solution.py:22
  2220.7 4.9 convert_element_type.259
  (305 shorter events, 168.5 us)
Async XLA Ops:
  7.2 53.4 %copy-start = (bf16[768,1536]{1,0:T(8,128)(2,1)S(1)}, bf16[768,1536]{1,0:T(8,128)(2,1)}, u32[]{:S(2)}) copy-start(bf16[768,1536]{1,0:T(8,128)(2,1)} %param.10) | copy-start | bytes 7077892
  7.2 100.5 %reduce-scatter.5.cloned.1.call-start = ((), (), s32[]{:S(2)}) async-start(), calls=%async_computation.4 | async-start | bytes 2875392 | tf_op jit(solution)/shard_map/reduce_scatter | solution.py:149
  8.1 20.7 copy-start.59
  8.1 36.9 %copy-start.49 = (f32[768]{0:T(1024)}, f32[768]{0:T(1024)S(1)}, u32[]{:S(2)}) copy-start(f32[768]{0:T(1024)S(1)} %get-tuple-element.65) | copy-start | bytes 9220
  10.5 3.4 copy-start.75
  10.5 3.5 copy-start.1
  10.5 6.3 copy-start.17
  13.9 14.9 copy-start.76
  16.9 12.0 copy-start.61
  17.8 11.1 copy-start.69
  39.5 3.8 copy-start.4
  39.6 3.8 copy-start.45
  43.3 28.7 %copy-start.32 = (bf16[12,64,312]{2,1,0:T(8,128)(2,1)}, bf16[12,64,312]{2,1,0:T(8,128)(2,1)S(1)}, u32[]{:S(2)}) copy-start(bf16[12,64,312]{2,1,0:T(8,128)(2,1)S(1)} %fusion.49) | copy-start | bytes 1437700
  44.0 63.6 %copy-start.9 = (f32[312,768]{1,0:T(8,128)}, f32[312,768]{1,0:T(8,128)S(1)}, u32[]{:S(2)}) copy-start(f32[312,768]{1,0:T(8,128)S(1)} %get-tuple-element.74) | copy-start | bytes 2875396
  60.6 11.4 copy-start.40
  60.6 12.7 copy-start.80
  76.2 205.5 %all-gather.6.cloned.1.call-start = ((), (), s32[]{:S(2)}) async-start(), calls=%async_computation.5 | async-start | bytes 4718592 | tf_op jit(solution)/shard_map/all_gather | solution.py:176
  92.9 24.0 %copy-start.67 = (f32[512]{0:T(512)}, f32[512]{0:T(512)S(1)}, u32[]{:S(2)}) copy-start(f32[512]{0:T(512)S(1)} %get-tuple-element.63) | copy-start | bytes 6148
  92.9 21.1 copy-start.65
  114.1 8.0 copy-start.47
  116.9 5.1 copy-start.55
  188.1 7.5 copy-start.22
  195.6 10.3 copy-start.28
  223.0 6.9 copy-start.34
  236.6 91.6 %all-gather.8.cloned.1.call-start = ((), (), s32[]{:S(2)}) async-start(), calls=%async_computation.7 | async-start | bytes 4718592 | tf_op jit(solution)/shard_map/all_gather | solution.py:182
  237.4 156.0 %reduce-scatter.9.cloned.1.call-start = ((), (), s32[]{:S(2)}) async-start(), calls=%async_computation.8 | async-start | bytes 4718592 | tf_op jit(solution)/shard_map/reduce_scatter | solution.py:186
  328.2 16.8 copy-start.82
  349.8 192.3 %reduce-scatter.7.cloned.1.call-start = ((), (), s32[]{:S(2)}) async-start(), calls=%async_computation.6 | async-start | bytes 4718592 | tf_op jit(solution)/shard_map/reduce_scatter | solution.py:179
  363.4 237.5 %reduce-scatter.11.cloned.1.call-start = ((), (), s32[]{:S(2)}) async-start(), calls=%async_computation.9 | async-start | bytes 1437696 | tf_op jit(solution)/shard_map/reduce_scatter | solution.py:222
  393.3 3.3 copy-start.3
  393.4 3.8 copy-start.11
  393.4 5.3 copy-start.14
  416.6 10.5 copy-start.6
  475.9 6.7 copy-start.5
  542.1 10.6 copy-start.77
  550.0 6.4 copy-start.29
  550.0 6.4 copy-start.78
  556.4 21.0 copy-start.39
  556.4 14.8 copy-start.81
  571.2 6.2 copy-start.42
  581.3 268.7 %all-reduce.5.cloned.1.call-start = ((), (), s32[]{:S(2)}) async-start(), calls=%async_computation.11 | async-start | bytes 15216640
  581.4 4.1 copy-start.8
  592.0 8.9 copy-start.10
  592.0 8.9 copy-start.50
  592.0 8.9 copy-start.54
  592.0 10.3 copy-start.74
  592.0 10.3 copy-start.64
  600.8 4.8 copy-start.21
  602.3 4.3 copy-start.33
  608.7 3.9 copy-start.16
  608.7 7.9 slice-start
  612.6 4.1 slice-start.1
  623.8 7.6 copy-start.72
  639.1 3.5 copy-start.26
  639.1 4.1 copy-start.25
  643.2 21.4 copy-start.36
  668.1 335.6 %all-reduce.7.cloned.1.call-start = ((), (), s32[]{:S(2)}) async-start(), calls=%async_computation.12 | async-start | bytes 13631488 | tf_op jit(solution)/shard_map/psum | solution.py:262
  668.2 8.3 copy-start.79
  676.5 7.4 copy-start.43
  676.5 7.4 copy-start.87
  683.9 3.5 copy-start.41
  683.9 3.5 copy-start.85
  690.9 898.3 %all-gather.10.cloned.1.call-start = ((), (), s32[]{:S(2)}) async-start(), calls=%async_computation.10 | async-start | bytes 129341440 | tf_op jit(solution)/shard_map/all_gather | solution.py:21
  1003.7 5.8 copy-start.31
  (36 other events, 70.9 us)
Sparse Core Ops, SparseCore 0:
  76.3 31.3 reduce-scatter.4
  236.7 44.8 all-gather.5
  283.2 44.9 all-gather.7
  350.0 43.3 reduce-scatter.8
  395.5 43.3 reduce-scatter.6
  581.4 19.3 reduce-scatter.10
  668.2 181.6 all-reduce.4
  854.6 149.0 all-reduce.6
  1005.9 583.1 all-gather.9
